TPU v7x, 32 devices: a whole 2x2x4 slice. The times are simulated.
32 devices in a mesh: scan: 16 (over z, y, x), col: 2 (over core).
Axes of the slice: x: 2, y: 2, z: 4, core: 2. Of those that a mesh axis runs over, the one named last changes fastest.
Arguments:
- frames: float32 [256, 128, 2048], P('scan', None, 'col'), may hold values from -6 to 6
- depth_offset: int32 [128], replicated, may hold values from -64 to 64
- band_width: int32 [128], replicated, may hold values from 1 to 8
- edge_level: int32 [128, 2048], P(None, 'col'), may hold values from 1 to 16
Outputs:
- volume: float32 [256, 128, 2048], P('scan', None, 'col')
All inputs are finite; a program needn't handle non-finite values.
Results may differ from a plain program's by a relative error of at most 0.0003.
Values sent between devices are 32-bit elements; how exact they have to be, the bound alone decides.
A program may use at most 128 MiB of HBM per device.

v0:
```python
import math

import jax
import jax.numpy as jnp
from jax import lax
from jax.sharding import PartitionSpec as P

SWEEPS = 6
DIFFUSE = 6


TEMPORAL_KAPPA = 1.0
STEP_SIZE = 0.24
LEVEL_SCALE = 16.0


def with_halo(shard, sides, width):
    for axis, dim in sides:
        size, length = (lax.axis_size(axis), shard.shape[dim])
        up = [(i, (i + 1) % size) for i in range(size - 1)]
        down = [(j, i) for i, j in up]
        last = lax.slice_in_dim(shard, length - width, length, axis=dim)
        initial = lax.slice_in_dim(shard, 0, width, axis=dim)
        before = lax.ppermute(last, axis, up)
        after = lax.ppermute(initial, axis, down)
        shard = jnp.concatenate([before, shard, after], axis=dim)
    return shard


def diffuse_once(field, kappa, live_mask):
    change = (field[1:] - field[:-1]) * (live_mask[1:] * live_mask[:-1])
    flux_out = change / (1.0 + change * change / (kappa * kappa))
    zero_row = jnp.zeros_like(flux_out[:1])
    return field + STEP_SIZE * (
        jnp.concatenate([flux_out, zero_row], 0) - jnp.concatenate([zero_row, flux_out], 0)
    )


def diffuse_steps(field, kappa, live_mask, step_count):
    for sweep_no in range(step_count):
        field = diffuse_once(field, kappa, live_mask)
    return field


def live_frames(my_index, local_count, halo_width, all_count):
    position = (
        my_index * local_count
        - halo_width
        + jnp.arange(local_count + 2 * halo_width, dtype=jnp.int32)
    )
    inside = (position >= 0) & (position < all_count)
    return inside.astype(jnp.float32)[:, None, None]


def resample_rows(wire_signal, row_offsets, widths):
    depth_count = wire_signal.shape[0]
    block_rows = math.gcd(depth_count, 512)
    frame_index = jnp.arange(depth_count, dtype=jnp.int32)[None, None, :]
    weights = (1.0 / widths.astype(jnp.float32))[:, None, None]

    def one_block(first_depth):
        depth_index = first_depth + jnp.arange(block_rows, dtype=jnp.int32)[None, :, None]
        spacing = depth_index - frame_index - row_offsets[:, None, None]
        band_rows = jnp.where((spacing >= 0) & (spacing < widths[:, None, None]), weights, 0.0)
        return jnp.einsum("rdw,wrc->drc", band_rows, wire_signal, precision=lax.Precision.HIGHEST)

    starts = jnp.arange(depth_count // block_rows, dtype=jnp.int32) * block_rows
    pieces = lax.map(one_block, starts)
    return pieces.reshape(depth_count, wire_signal.shape[1], wire_signal.shape[2])


def body(frames, depth_offset, band_width, edge_level):
    local_frames = frames.shape[0]
    scan_count = lax.axis_size("scan")
    my_index = lax.axis_index("scan")
    all_frames = local_frames * scan_count
    rows_dev = frames.shape[1] // scan_count
    plane_rows = lax.all_to_all(frames, "scan", split_axis=1, concat_axis=0, tiled=True)
    full_mask = jnp.ones((all_frames, 1, 1), jnp.float32)
    plane_rows = diffuse_steps(plane_rows, TEMPORAL_KAPPA, full_mask, SWEEPS)
    wire_signal = jnp.concatenate(
        [plane_rows[:-1] - plane_rows[1:], jnp.zeros_like(plane_rows[:1])], 0
    )
    first_row = my_index * rows_dev
    row_offsets = lax.dynamic_slice_in_dim(depth_offset, first_row, rows_dev, 0)
    widths = lax.dynamic_slice_in_dim(band_width, first_row, rows_dev, 0)
    profile = resample_rows(wire_signal, row_offsets, widths)
    edge_scale = edge_level.astype(jnp.float32) / LEVEL_SCALE
    volume = lax.all_to_all(profile, "scan", split_axis=0, concat_axis=1, tiled=True)
    pixel_scale = edge_scale[None]
    edge_mask = live_frames(my_index, local_frames, 1, all_frames)
    for sweep_no in range(DIFFUSE):
        padded = with_halo(volume, (("scan", 0),), 1)
        volume = diffuse_steps(padded, pixel_scale, edge_mask, 1)[1 : 1 + local_frames]
    return volume


def solution(mesh):
    placed = (P("scan", None, "col"), P(), P(), P(None, "col"))
    return jax.shard_map(
        body, mesh=mesh, in_specs=placed, out_specs=P("scan", None, "col"), check_vma=False
    )
```

profile of v0, /device:TPU:24, one launch (start us, length us, event | category | flops | bytes accessed | tf_op | source)
XLA Modules:
  0.0 766.7 jit_solution(4354026028091079480)
XLA Ops:
  0.0 11.6 %copy.19 = f32[16,128,1024]{2,0,1:T(8,128)} copy(f32[16,128,1024]{2,1,0:T(8,128)} %param.4) | data formatting | bytes 16777216 | tf_op args[0]
  11.6 7.5 all-to-all-start
  19.3 179.9 %all-to-all-done = f32[16,128,1024]{2,0,1:T(8,128)} async-done(((f32[16,128,1024]{2,0,1:T(8,128)}), f32[16,128,1024]{2,0,1:T(8,128)}, u32[]{:S(2)}, u32[]{:S(2)}) %all-to-all-start) | async-done | bytes 8388640 | tf_op jit(solution)/shard_map/all_to_all | solution.py:78
  199.3 13.9 %copy.21 = f32[16,16,8,1024]{3,2,1,0:T(8,128)} copy(f32[16,16,8,1024]{3,1,2,0:T(8,128)} %bitcast.2) | data formatting | bytes 16777216 | tf_op jit(solution)/shard_map/all_to_all | solution.py:78
  213.2 9.2 %copy.24 = f32[256,8,1024]{0,2,1:T(8,128)} copy(f32[256,8,1024]{2,1,0:T(8,128)} %bitcast.18) | data formatting | bytes 16777216 | tf_op jit(solution)/shard_map/all_to_all | solution.py:78
  222.4 10.3 %add_divide_fusion.11 = f32[255,8,1024]{0,2,1:T(8,128)} fusion(f32[256,8,1024]{0,2,1:T(8,128)} %copy.24), kind=kLoop, calls=%fused_computation.49 | loop fusion | flops 8355840 | bytes 25067520 | tf_op jit(solution)/shard_map/div | solution.py:32
  232.7 8.6 %multiply_add_fusion.5 = f32[256,8,1024]{0,2,1:T(8,128)S(1)} fusion(f32[256,8,1024]{0,2,1:T(8,128)S(1)} %copy-done, f32[255,8,1024]{0,2,1:T(8,128)} %add_divide_fusion.11), kind=kLoop, calls=%fused_computation.48 | loop fusion | flops 6291456 | bytes 25133056 | tf_op jit(solution)/shard_map/add | solution.py:34
  241.3 4.6 add_divide_fusion.10
  245.8 9.0 %multiply_add_fusion.4 = f32[256,8,1024]{0,2,1:T(8,128)S(1)} fusion(f32[256,8,1024]{0,2,1:T(8,128)S(1)} %multiply_add_fusion.5, f32[255,8,1024]{0,2,1:T(8,128)} %add_divide_fusion.10), kind=kLoop, calls=%fused_computation.46 | loop fusion | flops 6291456 | bytes 25133056 | tf_op jit(solution)/shard_map/add | solution.py:34
  254.8 4.6 add_divide_fusion.9
  259.4 8.6 %multiply_add_fusion.3 = f32[256,8,1024]{0,2,1:T(8,128)S(1)} fusion(f32[256,8,1024]{0,2,1:T(8,128)S(1)} %multiply_add_fusion.4, f32[255,8,1024]{0,2,1:T(8,128)} %add_divide_fusion.9), kind=kLoop, calls=%fused_computation.44 | loop fusion | flops 6291456 | bytes 25133056 | tf_op jit(solution)/shard_map/add | solution.py:34
  272.6 8.6 %multiply_add_fusion.2 = f32[256,8,1024]{0,2,1:T(8,128)S(1)} fusion(f32[256,8,1024]{0,2,1:T(8,128)S(1)} %multiply_add_fusion.3, f32[255,8,1024]{0,2,1:T(8,128)} %add_divide_fusion.8), kind=kLoop, calls=%fused_computation.42 | loop fusion | flops 6291456 | bytes 25133056 | tf_op jit(solution)/shard_map/add | solution.py:34
  285.7 8.6 %multiply_add_fusion.1 = f32[256,8,1024]{0,2,1:T(8,128)S(1)} fusion(f32[256,8,1024]{0,2,1:T(8,128)S(1)} %multiply_add_fusion.2, f32[255,8,1024]{0,2,1:T(8,128)} %add_divide_fusion.7), kind=kLoop, calls=%fused_computation.40 | loop fusion | flops 6291456 | bytes 25133056 | tf_op jit(solution)/shard_map/add | solution.py:34
  296.7 4.9 multiply_add_fusion
  301.6 11.3 %slice_subtract_fusion = f32[255,8,1024]{0,2,1:T(8,128)} fusion(f32[256,8,1024]{0,2,1:T(8,128)} %multiply_add_fusion), kind=kLoop, calls=%fused_computation.28 | loop fusion | flops 2088960 | bytes 25067520 | tf_op jit(solution)/shard_map/sub | solution.py:82
  312.8 12.3 %fusion.10 = f32[256,8,1024]{0,2,1:T(8,128)} fusion(f32[255,8,1024]{0,2,1:T(8,128)} %slice_subtract_fusion, f32[8]{0:T(128)S(1)} %get-tuple-element.17, s32[8]{0:T(128)S(1)} %get-tuple-element.18, s32[8]{0:T(128)S(1)} %dynamic_slice.9, s32[256,256]{1,0:T(8,128)S(1)} %iota_subtract_fusion), kind=kOutput, calls=%fused_computation.50 | convolution fusion | flops 6445072384 | bytes 17006688 | tf_op jit(solution)/shard_map/while/body/eval_jaxpr/rdw,wrc->drc/dot_general | solution.py:65
  325.2 8.9 %copy.25 = f32[256,8,1024]{2,1,0:T(8,128)} copy(f32[256,8,1024]{0,2,1:T(8,128)} %fusion.10) | data formatting | bytes 16777216 | tf_op jit(solution)/shard_map/while/body/eval_jaxpr/rdw,wrc->drc/transpose | solution.py:65
  334.1 16.0 %all-to-all-start.1 = ((f32[256,8,1024]{2,1,0:T(8,128)}), f32[256,8,1024]{2,1,0:T(8,128)}, u32[]{:S(2)}, u32[]{:S(2)}) async-start(f32[256,8,1024]{2,1,0:T(8,128)} %copy.25), calls=%async_computation.1 | async-start | bytes 16777216 | tf_op jit(solution)/shard_map/all_to_all | solution.py:89
  350.1 178.7 %all-to-all-done.1 = f32[256,8,1024]{2,1,0:T(8,128)} async-done(((f32[256,8,1024]{2,1,0:T(8,128)}), f32[256,8,1024]{2,1,0:T(8,128)}, u32[]{:S(2)}, u32[]{:S(2)}) %all-to-all-start.1) | async-done | bytes 8388640 | tf_op jit(solution)/shard_map/all_to_all | solution.py:89
  531.9 5.9 collective-permute-start.1
  542.3 4.9 collective-permute-done
  547.2 16.9 %collective-permute-done.1 = f32[1,128,1024]{2,1,0:T(8,128)S(1)} collective-permute-done((f32[1,128,1024]{2,1,0:T(8,128)S(1)}, f32[1,128,1024]{2,1,0:T(8,128)S(1)}, u32[]{:S(2)}, u32[]{:S(2)}) %collective-permute-start.1) | collective-permute-done | bytes 524320 | tf_op jit(solution)/shard_map/ppermute | solution.py:25
  564.1 4.7 add_divide_fusion.5
  568.8 7.8 %maximum_add_fusion = f32[18,128,1024]{2,1,0:T(8,128)S(1)} fusion(f32[1,128,1024]{2,1,0:T(8,128)S(1)} %collective-permute-done.1, f32[16,128,1024]{2,1,0:T(8,128)S(1)} %bitcast.17, f32[1,128,1024]{2,1,0:T(8,128)S(1)} %collective-permute-done, f32[17,128,1024]{2,1,0:T(8,128)} %add_divide_fusion.5), kind=kLoop, calls=%fused_computation | loop fusion | flops 11796480 | bytes 27787264 | tf_op jit(solution)/shard_map/add | solution.py:34
  579.0 5.7 collective-permute-start.3
  586.3 4.8 collective-permute-done.2
  591.1 8.2 %collective-permute-done.3 = f32[1,128,1024]{2,1,0:T(8,128)S(1)} collective-permute-done((f32[1,128,1024]{2,1,0:T(8,128)S(1)}, f32[1,128,1024]{2,1,0:T(8,128)S(1)}, u32[]{:S(2)}, u32[]{:S(2)}) %collective-permute-start.3) | collective-permute-done | bytes 524320 | tf_op jit(solution)/shard_map/ppermute | solution.py:25
  599.3 4.7 add_divide_fusion.4
  603.9 7.8 %maximum_add_fusion.1 = f32[18,128,1024]{2,1,0:T(8,128)S(1)} fusion(f32[1,128,1024]{2,1,0:T(8,128)S(1)} %collective-permute-done.3, f32[16,128,1024]{2,1,0:T(8,128)S(1)} %slice.207, f32[1,128,1024]{2,1,0:T(8,128)S(1)} %collective-permute-done.2, f32[17,128,1024]{2,1,0:T(8,128)} %add_divide_fusion.4), kind=kLoop, calls=%fused_computation.1 | loop fusion | flops 11796480 | bytes 27787264 | tf_op jit(solution)/shard_map/add | solution.py:34
  613.8 5.7 collective-permute-start.5
  621.2 6.2 collective-permute-done.4
  627.4 10.8 %collective-permute-done.5 = f32[1,128,1024]{2,1,0:T(8,128)S(1)} collective-permute-done((f32[1,128,1024]{2,1,0:T(8,128)S(1)}, f32[1,128,1024]{2,1,0:T(8,128)S(1)}, u32[]{:S(2)}, u32[]{:S(2)}) %collective-permute-start.5) | collective-permute-done | bytes 524320 | tf_op jit(solution)/shard_map/ppermute | solution.py:25
  638.3 4.7 add_divide_fusion.3
  642.9 7.8 %maximum_add_fusion.2 = f32[18,128,1024]{2,1,0:T(8,128)S(1)} fusion(f32[1,128,1024]{2,1,0:T(8,128)S(1)} %collective-permute-done.5, f32[16,128,1024]{2,1,0:T(8,128)S(1)} %slice.210, f32[1,128,1024]{2,1,0:T(8,128)S(1)} %collective-permute-done.4, f32[17,128,1024]{2,1,0:T(8,128)} %add_divide_fusion.3), kind=kLoop, calls=%fused_computation.2 | loop fusion | flops 11796480 | bytes 27787264 | tf_op jit(solution)/shard_map/add | solution.py:34
  653.1 5.8 collective-permute-start.7
  660.6 7.5 collective-permute-done.6
  668.1 10.0 %collective-permute-done.7 = f32[1,128,1024]{2,1,0:T(8,128)S(1)} collective-permute-done((f32[1,128,1024]{2,1,0:T(8,128)S(1)}, f32[1,128,1024]{2,1,0:T(8,128)S(1)}, u32[]{:S(2)}, u32[]{:S(2)}) %collective-permute-start.7) | collective-permute-done | bytes 524320 | tf_op jit(solution)/shard_map/ppermute | solution.py:25
  678.1 4.7 add_divide_fusion.2
  682.8 7.8 %maximum_add_fusion.3 = f32[18,128,1024]{2,1,0:T(8,128)S(1)} fusion(f32[1,128,1024]{2,1,0:T(8,128)S(1)} %collective-permute-done.7, f32[16,128,1024]{2,1,0:T(8,128)S(1)} %slice.213, f32[1,128,1024]{2,1,0:T(8,128)S(1)} %collective-permute-done.6, f32[17,128,1024]{2,1,0:T(8,128)} %add_divide_fusion.2), kind=kLoop, calls=%fused_computation.3 | loop fusion | flops 11796480 | bytes 27787264 | tf_op jit(solution)/shard_map/add | solution.py:34
  693.0 5.4 collective-permute-start.9
  700.1 7.5 collective-permute-done.8
  707.6 11.3 %collective-permute-done.9 = f32[1,128,1024]{2,1,0:T(8,128)S(1)} collective-permute-done((f32[1,128,1024]{2,1,0:T(8,128)S(1)}, f32[1,128,1024]{2,1,0:T(8,128)S(1)}, u32[]{:S(2)}, u32[]{:S(2)}) %collective-permute-start.9) | collective-permute-done | bytes 524320 | tf_op jit(solution)/shard_map/ppermute | solution.py:25
  718.8 4.7 add_divide_fusion.1
  723.5 7.8 %maximum_add_fusion.4 = f32[18,128,1024]{2,1,0:T(8,128)S(1)} fusion(f32[1,128,1024]{2,1,0:T(8,128)S(1)} %collective-permute-done.9, f32[16,128,1024]{2,1,0:T(8,128)S(1)} %slice.216, f32[1,128,1024]{2,1,0:T(8,128)S(1)} %collective-permute-done.8, f32[17,128,1024]{2,1,0:T(8,128)} %add_divide_fusion.1), kind=kLoop, calls=%fused_computation.4 | loop fusion | flops 11796480 | bytes 27787264 | tf_op jit(solution)/shard_map/add | solution.py:34
  733.7 5.4 collective-permute-start.11
  740.8 7.5 collective-permute-done.10
  748.3 10.0 %collective-permute-done.11 = f32[1,128,1024]{2,1,0:T(8,128)S(1)} collective-permute-done((f32[1,128,1024]{2,1,0:T(8,128)S(1)}, f32[1,128,1024]{2,1,0:T(8,128)S(1)}, u32[]{:S(2)}, u32[]{:S(2)}) %collective-permute-start.11) | collective-permute-done | bytes 524320 | tf_op jit(solution)/shard_map/ppermute | solution.py:25
  761.2 5.1 fusion.6
  (36 shorter events, 41.6 us)
Async XLA Ops:
  11.6 7.5 copy-start.3
  11.6 7.6 copy-start.2
  11.6 187.6 %all-to-all-start = ((f32[16,128,1024]{2,0,1:T(8,128)}), f32[16,128,1024]{2,0,1:T(8,128)}, u32[]{:S(2)}, u32[]{:S(2)}) async-start(f32[16,128,1024]{2,0,1:T(8,128)} %copy.19), calls=%async_computation | async-start | bytes 16777216 | tf_op jit(solution)/shard_map/all_to_all | solution.py:78
  222.4 10.3 %copy-start = (f32[256,8,1024]{0,2,1:T(8,128)S(1)}, f32[256,8,1024]{0,2,1:T(8,128)}, u32[]{:S(2)}) copy-start(f32[256,8,1024]{0,2,1:T(8,128)} %copy.24) | copy-start | bytes 25165828
  334.1 203.9 %copy-start.1 = (s32[128,1024]{1,0:T(8,128)S(1)}, s32[128,1024]{1,0:T(8,128)}, u32[]{:S(2)}) copy-start(s32[128,1024]{1,0:T(8,128)} %param.7) | copy-start | bytes 1572868
  334.1 194.7 %all-to-all-start.1 = ((f32[256,8,1024]{2,1,0:T(8,128)}), f32[256,8,1024]{2,1,0:T(8,128)}, u32[]{:S(2)}, u32[]{:S(2)}) async-start(f32[256,8,1024]{2,1,0:T(8,128)} %copy.25), calls=%async_computation.1 | async-start | bytes 16777216 | tf_op jit(solution)/shard_map/all_to_all | solution.py:89
  530.0 17.2 %collective-permute-start = (f32[1,128,1024]{2,1,0:T(8,128)S(1)}, f32[1,128,1024]{2,1,0:T(8,128)S(1)}, u32[]{:S(2)}, u32[]{:S(2)}) collective-permute-start(f32[1,128,1024]{2,1,0:T(8,128)S(1)} %get-tuple-element.38), channel_id=1, source_target_pairs={{0,2},{2,4},{4,6},{6,8},{8,10},{10,12},{12,14},{14,16},{16,18},{18... | collective-permute-start | bytes 1572872 | tf_op jit(solution)/shard_map/ppermute | solution.py:24
  531.9 32.2 %collective-permute-start.1 = (f32[1,128,1024]{2,1,0:T(8,128)S(1)}, f32[1,128,1024]{2,1,0:T(8,128)S(1)}, u32[]{:S(2)}, u32[]{:S(2)}) collective-permute-start(f32[1,128,1024]{2,1,0:T(8,128)S(1)} %get-tuple-element.39), channel_id=1, source_target_pairs={{2,0},{4,2},{6,4},{8,6},{10,8},{12,10},{14,12},{16,14},{18,16},{20... | collective-permute-start | bytes 1572872 | tf_op jit(solution)/shard_map/ppermute | solution.py:25
  576.8 14.3 %collective-permute-start.2 = (f32[1,128,1024]{2,1,0:T(8,128)S(1)}, f32[1,128,1024]{2,1,0:T(8,128)S(1)}, u32[]{:S(2)}, u32[]{:S(2)}) collective-permute-start(f32[1,128,1024]{2,1,0:T(8,128)S(1)} %get-tuple-element.36), channel_id=1, source_target_pairs={{0,2},{2,4},{4,6},{6,8},{8,10},{10,12},{12,14},{14,16},{16,18},{18... | collective-permute-start | bytes 1572872 | tf_op jit(solution)/shard_map/ppermute | solution.py:24
  579.0 20.3 %collective-permute-start.3 = (f32[1,128,1024]{2,1,0:T(8,128)S(1)}, f32[1,128,1024]{2,1,0:T(8,128)S(1)}, u32[]{:S(2)}, u32[]{:S(2)}) collective-permute-start(f32[1,128,1024]{2,1,0:T(8,128)S(1)} %get-tuple-element.37), channel_id=1, source_target_pairs={{2,0},{4,2},{6,4},{8,6},{10,8},{12,10},{14,12},{16,14},{18,16},{20... | collective-permute-start | bytes 1572872 | tf_op jit(solution)/shard_map/ppermute | solution.py:25
  611.9 15.5 %collective-permute-start.4 = (f32[1,128,1024]{2,1,0:T(8,128)S(1)}, f32[1,128,1024]{2,1,0:T(8,128)S(1)}, u32[]{:S(2)}, u32[]{:S(2)}) collective-permute-start(f32[1,128,1024]{2,1,0:T(8,128)S(1)} %get-tuple-element.34), channel_id=1, source_target_pairs={{0,2},{2,4},{4,6},{6,8},{8,10},{10,12},{12,14},{14,16},{16,18},{18... | collective-permute-start | bytes 1572872 | tf_op jit(solution)/shard_map/ppermute | solution.py:24
  613.8 24.4 %collective-permute-start.5 = (f32[1,128,1024]{2,1,0:T(8,128)S(1)}, f32[1,128,1024]{2,1,0:T(8,128)S(1)}, u32[]{:S(2)}, u32[]{:S(2)}) collective-permute-start(f32[1,128,1024]{2,1,0:T(8,128)S(1)} %get-tuple-element.35), channel_id=1, source_target_pairs={{2,0},{4,2},{6,4},{8,6},{10,8},{12,10},{14,12},{16,14},{18,16},{20... | collective-permute-start | bytes 1572872 | tf_op jit(solution)/shard_map/ppermute | solution.py:25
  650.9 17.2 %collective-permute-start.6 = (f32[1,128,1024]{2,1,0:T(8,128)S(1)}, f32[1,128,1024]{2,1,0:T(8,128)S(1)}, u32[]{:S(2)}, u32[]{:S(2)}) collective-permute-start(f32[1,128,1024]{2,1,0:T(8,128)S(1)} %get-tuple-element.32), channel_id=1, source_target_pairs={{0,2},{2,4},{4,6},{6,8},{8,10},{10,12},{12,14},{14,16},{16,18},{18... | collective-permute-start | bytes 1572872 | tf_op jit(solution)/shard_map/ppermute | solution.py:24
  653.1 25.1 %collective-permute-start.7 = (f32[1,128,1024]{2,1,0:T(8,128)S(1)}, f32[1,128,1024]{2,1,0:T(8,128)S(1)}, u32[]{:S(2)}, u32[]{:S(2)}) collective-permute-start(f32[1,128,1024]{2,1,0:T(8,128)S(1)} %get-tuple-element.33), channel_id=1, source_target_pairs={{2,0},{4,2},{6,4},{8,6},{10,8},{12,10},{14,12},{16,14},{18,16},{20... | collective-permute-start | bytes 1572872 | tf_op jit(solution)/shard_map/ppermute | solution.py:25
  690.8 16.8 %collective-permute-start.8 = (f32[1,128,1024]{2,1,0:T(8,128)S(1)}, f32[1,128,1024]{2,1,0:T(8,128)S(1)}, u32[]{:S(2)}, u32[]{:S(2)}) collective-permute-start(f32[1,128,1024]{2,1,0:T(8,128)S(1)} %get-tuple-element.28), channel_id=1, source_target_pairs={{0,2},{2,4},{4,6},{6,8},{8,10},{10,12},{12,14},{14,16},{16,18},{18... | collective-permute-start | bytes 1572872 | tf_op jit(solution)/shard_map/ppermute | solution.py:24
  693.0 25.9 %collective-permute-start.9 = (f32[1,128,1024]{2,1,0:T(8,128)S(1)}, f32[1,128,1024]{2,1,0:T(8,128)S(1)}, u32[]{:S(2)}, u32[]{:S(2)}) collective-permute-start(f32[1,128,1024]{2,1,0:T(8,128)S(1)} %get-tuple-element.30), channel_id=1, source_target_pairs={{2,0},{4,2},{6,4},{8,6},{10,8},{12,10},{14,12},{16,14},{18,16},{20... | collective-permute-start | bytes 1572872 | tf_op jit(solution)/shard_map/ppermute | solution.py:25
  731.5 16.8 %collective-permute-start.10 = (f32[1,128,1024]{2,1,0:T(8,128)S(1)}, f32[1,128,1024]{2,1,0:T(8,128)S(1)}, u32[]{:S(2)}, u32[]{:S(2)}) collective-permute-start(f32[1,128,1024]{2,1,0:T(8,128)S(1)} %get-tuple-element.19), channel_id=1, source_target_pairs={{0,2},{2,4},{4,6},{6,8},{8,10},{10,12},{12,14},{14,16},{16,18},{18... | collective-permute-start | bytes 1572872 | tf_op jit(solution)/shard_map/ppermute | solution.py:24
  733.7 24.6 %collective-permute-start.11 = (f32[1,128,1024]{2,1,0:T(8,128)S(1)}, f32[1,128,1024]{2,1,0:T(8,128)S(1)}, u32[]{:S(2)}, u32[]{:S(2)}) collective-permute-start(f32[1,128,1024]{2,1,0:T(8,128)S(1)} %get-tuple-element.20), channel_id=1, source_target_pairs={{2,0},{4,2},{6,4},{8,6},{10,8},{12,10},{14,12},{16,14},{18,16},{20... | collective-permute-start | bytes 1572872 | tf_op jit(solution)/shard_map/ppermute | solution.py:25
where the time goes:
time: 776 us; the launch traced here: 767 us
  waiting for transfers between devices  464 us (60%)
  other arithmetic  161 us (21%)
  starting transfers between devices  70.1 us (9%)
  local copies, waits for them, and re-layouts  58.1 us (7%)
  matrix products  12.3 us (2%)
    all_to_all x1, waiting for transfers between devices, body(): lax.all_to_all(frames, 'scan', split_axis=1, concat_axis=0, tiled=True)  180 us
    all_to_all x1, waiting for transfers between devices, body(): lax.all_to_all(profile, 'scan', split_axis=0, concat_axis=1, tiled=True)  179 us
    add x12, other arithmetic, diffuse_once(): field + STEP_SIZE * (jnp.concatenate([flux_out, zero_row], 0) - jnp.conca...  92.4 us
    ppermute x6, waiting for transfers between devices, with_halo(): after = lax.ppermute(initial, axis, down)  67.3 us
    div x12, other arithmetic, diffuse_once(): flux_out = change / (1.0 + change * change / (kappa * kappa))  57.2 us
    ppermute x6, waiting for transfers between devices, with_halo(): before = lax.ppermute(last, axis, up)  38.4 us
    ppermute x6, starting transfers between devices, with_halo(): after = lax.ppermute(initial, axis, down)  34 us
    all_to_all x2, local copies, waits for them, and re-layouts, body(): lax.all_to_all(frames, 'scan', split_axis=1, concat_axis=0, tiled=True)  23.1 us
  transfers between devices with their start and end apart: 14, of which 14 were waited for; matrix products, arithmetic and copies ran while one was open for 2% of the time, Pallas kernels for 0%

commit v1 on v0

v1 whole, which is shorter than its diff:
```python
import functools

import jax
import jax.numpy as jnp
from jax import lax
from jax.experimental import pallas as pl
from jax.experimental.pallas import tpu as pltpu
from jax.sharding import PartitionSpec as P

SWEEPS = 6
DIFFUSE = 6
BAND = 8
TEMPORAL_KAPPA = 1.0
STEP_SIZE = 0.24
LEVEL_SCALE = 16.0
LANES = 128
ROWS = 8
LEAD = 4
CHUNKS = 4
FAR_LO = DIFFUSE + BAND - 1
FAR_HI = DIFFUSE + 1


def sweep_pass(src, dst, sweeps, inverse, cols):
    n_in, n_out = src.shape[0], dst.shape[0]
    lag = n_in - n_out
    lead = lag // 2 + 2 * sweeps - 1
    streams = len(cols)

    def advance(t, carry):
        held, flux, made = carry
        at = jnp.minimum(t, n_in - 1)
        new_held, new_flux, new_made = [], [], []
        for s, col in enumerate(cols):
            fresh = src[at, :, pl.ds(col, LANES)]
            for level in range(sweeps):
                k = s * sweeps + level
                b = fresh if level == 0 else made[k - 1]
                a = held[k]
                c = b - a
                cc = c * c if inverse is None else c * c * inverse[s]
                f = c / (1.0 + cc)
                new_made.append(a + STEP_SIZE * (f - flux[k]))
                new_held.append(b)
                new_flux.append(f)
        return tuple(new_held), tuple(new_flux), tuple(new_made)

    def warm(t, carry):
        return advance(t, carry)

    def work(t, carry):
        carry = advance(t + lead, carry)
        for s, col in enumerate(cols):
            dst[t, :, pl.ds(col, LANES)] = carry[2][s * sweeps + sweeps - 1]
        return carry

    start = tuple(src[0, :, pl.ds(col, LANES)] for col in cols for _ in range(sweeps))
    init = (start, start, start)
    carry = lax.fori_loop(0, lead, warm, init)
    lax.fori_loop(0, n_out, work, carry, unroll=2)


def column_groups(width):
    cols = list(range(0, width, LANES))
    return [cols[i : i + 2] for i in range(0, len(cols), 2)]


def smooth_kernel(where_ref, own, lo, hi, out, ext):
    frames, width = own.shape[0], own.shape[2]
    first = where_ref[1] == 0
    last = where_ref[1] == LEAD - 1
    for i in range(SWEEPS):
        ext[i] = jnp.where(first, own[SWEEPS - 1 - i], lo[i])
        ext[SWEEPS + frames + i] = jnp.where(last, own[frames - 1 - i], hi[i])

    def put(i, _):
        ext[SWEEPS + i] = own[i]
        return 0

    lax.fori_loop(0, frames, put, 0, unroll=8)
    for cols in column_groups(width):
        sweep_pass(ext, out, SWEEPS, None, cols)


def depth_kernel(where_ref, off_ref, bw_ref, far_lo, lo, own, hi, far_hi, edge, out, win, prof):
    frames, width = own.shape[0], own.shape[2]
    all_frames = frames * LEAD
    z = where_ref[1]
    row0 = (where_ref[0] * pl.num_programs(0) + pl.program_id(0)) * ROWS
    base = 0
    for part in (far_lo, lo, own, hi, far_hi):
        count = part.shape[0]
        if count < 16:
            for i in range(count):
                win[base + i] = part[i]
        else:

            def put(i, _, part=part, base=base):
                win[base + i] = part[i]
                return 0

            lax.fori_loop(0, count, put, 0, unroll=8)
        base += count
    origin = FAR_LO + frames - z * frames
    sub = lax.broadcasted_iota(jnp.int32, (ROWS, LANES), 0)
    offs = [off_ref[row0 + r] for r in range(ROWS)]
    bws = [bw_ref[row0 + r] for r in range(ROWS)]
    widths = jnp.full((ROWS, LANES), 1.0, jnp.float32)
    for r in range(ROWS):
        widths = jnp.where(sub == r, bws[r].astype(jnp.float32), widths)
    masks = [sub == r for r in range(ROWS)]

    def fill(d, _):
        depth = z * frames + d - DIFFUSE
        depth = jnp.where(depth < 0, -1 - depth, depth)
        depth = jnp.where(depth >= all_frames, 2 * all_frames - 1 - depth, depth)
        at_a, at_b = [], []
        for r in range(ROWS):
            at = depth - offs[r] + 1
            at_b.append(jnp.clip(at, 0, all_frames - 1) + origin)
            at_a.append(jnp.clip(at - bws[r], 0, all_frames - 1) + origin)
        for col in range(0, width, LANES):
            lanes = pl.ds(col, LANES)
            a = win[at_a[0], :, lanes]
            b = win[at_b[0], :, lanes]
            for r in range(1, ROWS):
                a = jnp.where(masks[r], win[at_a[r], :, lanes], a)
                b = jnp.where(masks[r], win[at_b[r], :, lanes], b)
            prof[d, :, lanes] = (a - b) / widths
        return 0

    lax.fori_loop(0, frames + 2 * DIFFUSE, fill, 0)
    for cols in column_groups(width):
        inverse = []
        for col in cols:
            level = edge[:, pl.ds(col, LANES)].astype(jnp.float32) / LEVEL_SCALE
            inverse.append(1.0 / (level * level))
        sweep_pass(prof, out, DIFFUSE, inverse, cols)


def smooth(where, own, lo, hi):
    frames, rows, width = own.shape

    def spec(count):
        return pl.BlockSpec((count, ROWS, width), lambda i, w: (0, i, 0))

    return pl.pallas_call(
        smooth_kernel,
        out_shape=jax.ShapeDtypeStruct(own.shape, own.dtype),
        grid_spec=pltpu.PrefetchScalarGridSpec(
            num_scalar_prefetch=1,
            grid=(rows // ROWS,),
            in_specs=[spec(frames), spec(SWEEPS), spec(SWEEPS)],
            out_specs=spec(frames),
            scratch_shapes=[pltpu.VMEM((frames + 2 * SWEEPS, ROWS, width), jnp.float32)],
        ),
        cost_estimate=pl.CostEstimate(
            flops=own.size * 100, bytes_accessed=own.size * 8, transcendentals=0
        ),
    )(where, own, lo, hi)


def depth(where, off, bw, far_lo, lo, own, hi, far_hi, edge, chunk):
    frames, rows, width = own.shape
    tiles = rows // ROWS

    def spec(count):
        return pl.BlockSpec((count, ROWS, width), lambda i, w, o, b: (0, i, 0))

    return pl.pallas_call(
        depth_kernel,
        out_shape=jax.ShapeDtypeStruct(own.shape, own.dtype),
        grid_spec=pltpu.PrefetchScalarGridSpec(
            num_scalar_prefetch=3,
            grid=(tiles,),
            in_specs=[
                spec(FAR_LO),
                spec(frames),
                spec(frames),
                spec(frames),
                spec(FAR_HI),
                pl.BlockSpec((ROWS, width), lambda i, w, o, b: (w[0] * tiles + i, chunk)),
            ],
            out_specs=spec(frames),
            scratch_shapes=[
                pltpu.VMEM((3 * frames + FAR_LO + FAR_HI, ROWS, width), jnp.float32),
                pltpu.VMEM((frames + 2 * DIFFUSE, ROWS, width), jnp.float32),
            ],
        ),
        cost_estimate=pl.CostEstimate(
            flops=own.size * 150, bytes_accessed=own.size * 20, transcendentals=0
        ),
    )(where, off, bw, far_lo, lo, own, hi, far_hi, edge)


def body(frames, depth_offset, band_width, edge_level):
    scan = lax.axis_size("scan")
    group = scan // LEAD
    me = lax.axis_index("scan")
    where = jnp.stack([me % group, me // group]).astype(jnp.int32)
    groups = [[z * group + k for k in range(group)] for z in range(LEAD)]
    cols = frames.shape[2]
    width = max(LANES, cols // CHUNKS)

    def move(value, step):
        pairs = [(i, i + step * group) for i in range(scan) if 0 <= i + step * group < scan]
        return lax.ppermute(value, "scan", pairs)

    pieces = []
    for chunk in range(cols // width):
        part = lax.slice_in_dim(frames, chunk * width, (chunk + 1) * width, axis=2)
        own = lax.all_to_all(
            part, "scan", split_axis=1, concat_axis=0, tiled=True, axis_index_groups=groups
        )
        lo = move(own[-SWEEPS:], 1)
        hi = move(own[:SWEEPS], -1)
        own = smooth(where, own, lo, hi)
        below = move(own, 1)
        above = move(own, -1)
        far_lo = move(own[-FAR_LO:], 2)
        far_hi = move(own[:FAR_HI], -2)
        made = depth(
            where, depth_offset, band_width, far_lo, below, own, above, far_hi, edge_level, chunk
        )
        made = lax.all_to_all(
            made, "scan", split_axis=0, concat_axis=1, tiled=True, axis_index_groups=groups
        )
        pieces.append(made)
    return jnp.concatenate(pieces, axis=2)


def solution(mesh):
    placed = (P("scan", None, "col"), P(), P(), P(None, "col"))
    return jax.shard_map(
        body, mesh=mesh, in_specs=placed, out_specs=P("scan", None, "col"), check_vma=False
    )
```

time: 776 us -> 547 us (0.70)
  waiting for transfers between devices: 464 us -> 217 us
  other arithmetic: 161 us -> 5.31 us
  Pallas kernels: 0 us -> 151 us
  starting transfers between devices: 70.1 us -> 108 us
  matrix products: 12.3 us -> 0 us
    all_to_all x2 -> x8, waiting for transfers between devices: 359 us -> 48.3 us  [the longest x4 41 us: body(): lax.all_to_all(part, 'scan', split_axis=1, concat_axis=0, tiled=True, axi...]
    pallas_call x0 -> x8, Pallas kernels: none -> 151 us  [the longest x4 108 us: depth(): pl.pallas_call(depth_kernel, out_shape=jax.ShapeDtypeStruct(own.shape, ow...]
    add x12 -> x0, other arithmetic: 92.4 us -> none  [diffuse_once(): field + STEP_SIZE * (jnp.concatenate([flux_out, zero_row], 0) - jnp.conca...]
    ppermute x12 -> x24, waiting for transfers between devices: 106 us -> 168 us  [move(): return lax.ppermute(value, 'scan', pairs)]
    div x13 -> x0, other arithmetic: 57.3 us -> none  [the longest x12 57.2 us: diffuse_once(): flux_out = change / (1.0 + change * change / (kappa * kappa))]
    ppermute x12 -> x24, starting transfers between devices: 46.7 us -> 74.7 us  [move(): return lax.ppermute(value, 'scan', pairs)]
    unnamed x9 -> x52, local copies, waits for them, and re-layouts: 11.6 us -> 24.4 us
    dot_general x1 -> x0, matrix products: 12.3 us -> none  [one_block(): jnp.einsum('rdw,wrc->drc', band_rows, wire_signal, precision=lax.Precisio...]
  transfers between devices with their start and end apart: 14 -> 32, of which waited for: 14 -> 14; matrix products, arithmetic and copies ran while one was open for 2% -> 7% of each run, Pallas kernels for 0% -> 28%
where the time goes in v1:
time: 547 us; the launch traced here: 541 us
  waiting for transfers between devices  217 us (40%)
  Pallas kernels  151 us (28%)
  starting transfers between devices  108 us (20%)
  local copies, waits for them, and re-layouts  60 us (11%)
    ppermute x24, waiting for transfers between devices, move(): return lax.ppermute(value, 'scan', pairs)  168 us
    pallas_call x4, Pallas kernels, depth(): pl.pallas_call(depth_kernel, out_shape=jax.ShapeDtypeStruct(own.shape, ow...  108 us
    ppermute x24, starting transfers between devices, move(): return lax.ppermute(value, 'scan', pairs)  74.7 us
    pallas_call x4, Pallas kernels, smooth(): pl.pallas_call(smooth_kernel, out_shape=jax.ShapeDtypeStruct(own.shape, o...  42.7 us
    all_to_all x4, waiting for transfers between devices, body(): lax.all_to_all(part, 'scan', split_axis=1, concat_axis=0, tiled=True, axi...  41 us
    unnamed x52, local copies, waits for them, and re-layouts  24.4 us
    all_to_all x4, starting transfers between devices, body(): lax.all_to_all(made, 'scan', split_axis=0, concat_axis=1, tiled=True, axi...  17.4 us
    all_to_all x4, starting transfers between devices, body(): lax.all_to_all(part, 'scan', split_axis=1, concat_axis=0, tiled=True, axi...  16.2 us
  transfers between devices with their start and end apart: 32, of which 14 were waited for; matrix products, arithmetic and copies ran while one was open for 7% of the time, Pallas kernels for 28%

profile of v1, /device:TPU:24, one launch (start us, length us, event | category | flops | bytes accessed | tf_op | source)
XLA Modules:
  0.0 541.3 jit_solution(12250535066392964602)
XLA Ops:
  0.0 6.4 %fusion = (f32[16,128,256]{2,1,0:T(8,128)S(1)}, f32[16,128,256]{2,1,0:T(8,128)}, f32[16,128,256]{2,1,0:T(8,128)}, f32[16,128,256]{2,1,0:T(8,128)}) fusion(f32[16,128,1024]{2,1,0:T(8,128)} %param.4), kind=kLoop, calls=%fused_computation.2 | loop fusion | bytes 16777216 | tf_op jit(solution)/shard_map/slice | solution.py:211
  6.4 2.6 copy.25
  9.0 3.7 all-to-all-start
  12.7 4.2 copy.26
  16.9 20.9 %all-to-all-done = f32[16,128,256]{2,0,1:T(8,128)S(1)} async-done(((f32[16,128,256]{2,0,1:T(8,128)}), f32[16,128,256]{2,0,1:T(8,128)S(1)}, u32[]{:S(2)}, u32[]{:S(2)}) %all-to-all-start) | async-done | bytes 2097184 | tf_op jit(solution)/shard_map/all_to_all | solution.py:212
  39.0 3.6 all-to-all-start.2
  42.7 4.2 copy.27
  46.8 20.2 %all-to-all-done.2 = f32[16,128,256]{2,0,1:T(8,128)S(1)} async-done(((f32[16,128,256]{2,0,1:T(8,128)}), f32[16,128,256]{2,0,1:T(8,128)S(1)}, u32[]{:S(2)}, u32[]{:S(2)}) %all-to-all-start.2) | async-done | bytes 2097184 | tf_op jit(solution)/shard_map/all_to_all | solution.py:212
  68.4 4.4 all-to-all-start.4
  72.8 2.8 copy.14
  77.0 4.6 collective-permute-start.1
  85.4 10.7 %shard_map.46.own = f32[64,32,256]{2,1,0:T(8,128)} custom-call(s32[2]{0:T(128)} %pad_add_fusion.where_ref, f32[64,32,256]{2,1,0:T(8,128)} %bitcast.35, f32[6,32,256]{2,1,0:T(8,128)} %copy-done.16, f32[6,32,256]{2,1,0:T(8,128)} %copy-done.17), custom_call_target="tpu_custom_call" | custom-call | flops 52428800 | bytes 4194304 | tf_op jit(solution)/shard_map/pallas_call | solution.py:147
  97.3 6.4 %collective-permute-start.4 = (f32[64,32,256]{2,1,0:T(8,128)}, f32[64,32,256]{2,1,0:T(8,128)}, u32[]{:S(2)}, u32[]{:S(2)}) collective-permute-start(f32[64,32,256]{2,1,0:T(8,128)} %shard_map.46.own), channel_id=1, source_target_pairs={{8,0},{10,2},{12,4},{14,6},{16,8},{18,10},{20,12},{22,14},{24,16},... | collective-permute-start | bytes 6291464 | tf_op jit(solution)/shard_map/ppermute | solution.py:207
  103.7 4.1 copy.28
  107.8 4.5 all-to-all-start.6
  112.3 2.8 copy.17
  116.5 4.6 collective-permute-start.7
  122.0 3.8 collective-permute-start.5
  125.8 22.9 %collective-permute-done.6.lo = f32[6,32,256]{2,1,0:T(8,128)S(1)} collective-permute-done((f32[6,32,256]{2,1,0:T(8,128)S(1)}, f32[6,32,256]{2,1,0:T(8,128)S(1)}, u32[]{:S(2)}, u32[]{:S(2)}) %collective-permute-start.6) | collective-permute-done | bytes 196640 | tf_op jit(solution)/shard_map/ppermute | solution.py:207
  148.7 3.6 collective-permute-done.7.hi
  153.0 10.7 %shard_map.48.own = f32[64,32,256]{2,1,0:T(8,128)} custom-call(s32[2]{0:T(128)} %pad_add_fusion.where_ref, f32[64,32,256]{2,1,0:T(8,128)} %bitcast.37, f32[6,32,256]{2,1,0:T(8,128)} %copy-done.18, f32[6,32,256]{2,1,0:T(8,128)} %copy-done.21), custom_call_target="tpu_custom_call" | custom-call | flops 52428800 | bytes 4194304 | tf_op jit(solution)/shard_map/pallas_call | solution.py:147
  163.7 9.9 %collective-permute-start.10 = (f32[64,32,256]{2,1,0:T(8,128)}, f32[64,32,256]{2,1,0:T(8,128)}, u32[]{:S(2)}, u32[]{:S(2)}) collective-permute-start(f32[64,32,256]{2,1,0:T(8,128)} %shard_map.48.own), channel_id=1, source_target_pairs={{8,0},{10,2},{12,4},{14,6},{16,8},{18,10},{20,12},{22,14},{24,16},... | collective-permute-start | bytes 6291464 | tf_op jit(solution)/shard_map/ppermute | solution.py:207
  177.2 54.3 %collective-permute-done.2.far_lo = f32[13,32,256]{2,1,0:T(8,128)S(1)} collective-permute-done((f32[13,32,256]{2,1,0:T(8,128)S(1)}, f32[13,32,256]{2,1,0:T(8,128)S(1)}, u32[]{:S(2)}, u32[]{:S(2)}) %collective-permute-start.2) | collective-permute-done | bytes 426016 | tf_op jit(solution)/shard_map/ppermute | solution.py:207
  232.3 27.0 %shard_map.47 = f32[64,32,256]{2,1,0:T(8,128)} custom-call(s32[2]{0:T(128)} %pad_add_fusion.where_ref, s32[128]{0:T(128)} %off_ref.7, s32[128]{0:T(128)} %bw_ref.7, f32[13,32,256]{2,1,0:T(8,128)} %copy-done.9, f32[64,32,256]{2,1,0:T(8,128)} %collective-permute-done.3.lo, f32[64,32,256]{2,1,0:T(8,128)} %shard_map.46.own, ...), custom_call_target="tpu_custom_call" | custom-call | flops 78643200 | bytes 10485760 | tf_op jit(solution)/shard_map/pallas_call | solution.py:170
  259.3 4.6 all-to-all-start.1
  263.9 2.8 copy.20
  268.1 4.6 collective-permute-start.13
  276.5 10.7 %shard_map.50.own = f32[64,32,256]{2,1,0:T(8,128)} custom-call(s32[2]{0:T(128)} %pad_add_fusion.where_ref, f32[64,32,256]{2,1,0:T(8,128)} %bitcast.39, f32[6,32,256]{2,1,0:T(8,128)} %copy-done.19, f32[6,32,256]{2,1,0:T(8,128)} %copy-done.22), custom_call_target="tpu_custom_call" | custom-call | flops 52428800 | bytes 4194304 | tf_op jit(solution)/shard_map/pallas_call | solution.py:147
  288.5 6.4 %collective-permute-start.16 = (f32[64,32,256]{2,1,0:T(8,128)}, f32[64,32,256]{2,1,0:T(8,128)}, u32[]{:S(2)}, u32[]{:S(2)}) collective-permute-start(f32[64,32,256]{2,1,0:T(8,128)} %shard_map.50.own), channel_id=1, source_target_pairs={{8,0},{10,2},{12,4},{14,6},{16,8},{18,10},{20,12},{22,14},{24,16},... | collective-permute-start | bytes 6291464 | tf_op jit(solution)/shard_map/ppermute | solution.py:207
  297.2 42.5 %collective-permute-done.8.far_lo = f32[13,32,256]{2,1,0:T(8,128)S(1)} collective-permute-done((f32[13,32,256]{2,1,0:T(8,128)S(1)}, f32[13,32,256]{2,1,0:T(8,128)S(1)}, u32[]{:S(2)}, u32[]{:S(2)}) %collective-permute-start.8) | collective-permute-done | bytes 426016 | tf_op jit(solution)/shard_map/ppermute | solution.py:207
  340.4 27.0 %shard_map.49 = f32[64,32,256]{2,1,0:T(8,128)} custom-call(s32[2]{0:T(128)} %pad_add_fusion.where_ref, s32[128]{0:T(128)} %off_ref.7, s32[128]{0:T(128)} %bw_ref.7, f32[13,32,256]{2,1,0:T(8,128)} %copy-done.10, f32[64,32,256]{2,1,0:T(8,128)} %collective-permute-done.9.lo, f32[64,32,256]{2,1,0:T(8,128)} %shard_map.48.own, ...), custom_call_target="tpu_custom_call" | custom-call | flops 78643200 | bytes 10485760 | tf_op jit(solution)/shard_map/pallas_call | solution.py:170
  367.4 4.4 all-to-all-start.3
  371.9 2.8 copy.23
  376.0 4.6 collective-permute-start.19
  386.5 10.6 %shard_map.52.own = f32[64,32,256]{2,1,0:T(8,128)} custom-call(s32[2]{0:T(128)} %pad_add_fusion.where_ref, f32[64,32,256]{2,1,0:T(8,128)} %bitcast.41, f32[6,32,256]{2,1,0:T(8,128)} %copy-done.20, f32[6,32,256]{2,1,0:T(8,128)} %copy-done.23), custom_call_target="tpu_custom_call" | custom-call | flops 52428800 | bytes 4194304 | tf_op jit(solution)/shard_map/pallas_call | solution.py:147
  398.4 6.3 %collective-permute-start.22 = (f32[64,32,256]{2,1,0:T(8,128)}, f32[64,32,256]{2,1,0:T(8,128)}, u32[]{:S(2)}, u32[]{:S(2)}) collective-permute-start(f32[64,32,256]{2,1,0:T(8,128)} %shard_map.52.own), channel_id=1, source_target_pairs={{8,0},{10,2},{12,4},{14,6},{16,8},{18,10},{20,12},{22,14},{24,16},... | collective-permute-start | bytes 6291464 | tf_op jit(solution)/shard_map/ppermute | solution.py:207
  407.1 35.4 %collective-permute-done.14.far_lo = f32[13,32,256]{2,1,0:T(8,128)S(1)} collective-permute-done((f32[13,32,256]{2,1,0:T(8,128)S(1)}, f32[13,32,256]{2,1,0:T(8,128)S(1)}, u32[]{:S(2)}, u32[]{:S(2)}) %collective-permute-start.14) | collective-permute-done | bytes 426016 | tf_op jit(solution)/shard_map/ppermute | solution.py:207
  443.2 27.0 %shard_map.51 = f32[64,32,256]{2,1,0:T(8,128)} custom-call(s32[2]{0:T(128)} %pad_add_fusion.where_ref, s32[128]{0:T(128)} %off_ref.7, s32[128]{0:T(128)} %bw_ref.7, f32[13,32,256]{2,1,0:T(8,128)} %copy-done.11, f32[64,32,256]{2,1,0:T(8,128)} %collective-permute-done.15.lo, f32[64,32,256]{2,1,0:T(8,128)} %shard_map.50.own, ...), custom_call_target="tpu_custom_call" | custom-call | flops 78643200 | bytes 10485760 | tf_op jit(solution)/shard_map/pallas_call | solution.py:170
  470.3 3.9 all-to-all-start.5
  477.5 5.5 %collective-permute-start.23 = (f32[7,32,256]{2,1,0:T(8,128)S(1)}, f32[7,32,256]{2,1,0:T(8,128)S(1)}, u32[]{:S(2)}, u32[]{:S(2)}) collective-permute-start(f32[7,32,256]{2,1,0:T(8,128)S(1)} %slice.95), channel_id=1, source_target_pairs={{16,0},{18,2},{20,4},{22,6},{24,8},{26,10},{28,12},{30,14},{17,1},... | collective-permute-start | bytes 688136 | tf_op jit(solution)/shard_map/ppermute | solution.py:207
  483.0 3.5 collective-permute-done.23.far_hi
  487.3 26.9 %shard_map.53 = f32[64,32,256]{2,1,0:T(8,128)} custom-call(s32[2]{0:T(128)} %pad_add_fusion.where_ref, s32[128]{0:T(128)} %off_ref.7, s32[128]{0:T(128)} %bw_ref.7, f32[13,32,256]{2,1,0:T(8,128)} %copy-done.8, f32[64,32,256]{2,1,0:T(8,128)} %collective-permute-done.21.lo, f32[64,32,256]{2,1,0:T(8,128)} %shard_map.52.own, ...), custom_call_target="tpu_custom_call" | custom-call | flops 78643200 | bytes 10485760 | tf_op jit(solution)/shard_map/pallas_call | solution.py:170
  514.2 4.5 all-to-all-start.7
  518.7 3.2 copy.15
  521.9 3.2 copy.18
  526.6 7.2 %all-to-all-done.7 = f32[64,32,256]{2,1,0:T(8,128)} async-done(((f32[64,32,256]{2,1,0:T(8,128)}), f32[64,32,256]{2,1,0:T(8,128)}, u32[]{:S(2)}, u32[]{:S(2)}) %all-to-all-start.7) | async-done | bytes 2097184 | tf_op jit(solution)/shard_map/all_to_all | solution.py:225
  533.8 2.0 copy.24
  536.7 4.7 pad_maximum_fusion
  (99 shorter events, 44.0 us)
Async XLA Ops:
  9.0 28.7 %all-to-all-start = ((f32[16,128,256]{2,0,1:T(8,128)}), f32[16,128,256]{2,0,1:T(8,128)S(1)}, u32[]{:S(2)}, u32[]{:S(2)}) async-start(f32[16,128,256]{2,0,1:T(8,128)} %copy.25), calls=%async_computation | async-start | bytes 4194304 | tf_op jit(solution)/shard_map/all_to_all | solution.py:212
  37.7 1.3 copy-start.5
  39.0 28.0 %all-to-all-start.2 = ((f32[16,128,256]{2,0,1:T(8,128)}), f32[16,128,256]{2,0,1:T(8,128)S(1)}, u32[]{:S(2)}, u32[]{:S(2)}) async-start(f32[16,128,256]{2,0,1:T(8,128)} %copy.26), calls=%async_computation.2 | async-start | bytes 4194304 | tf_op jit(solution)/shard_map/all_to_all | solution.py:212
  67.0 1.4 copy-start.4
  68.4 39.4 %all-to-all-start.4 = ((f32[16,128,256]{2,0,1:T(8,128)}), f32[16,128,256]{2,0,1:T(8,128)}, u32[]{:S(2)}, u32[]{:S(2)}) async-start(f32[16,128,256]{2,0,1:T(8,128)} %copy.27), calls=%async_computation.4 | async-start | bytes 4194304 | tf_op jit(solution)/shard_map/all_to_all | solution.py:212
  75.6 9.1 %copy-start = (f32[16,4,32,256]{3,2,0,1:T(8,128)}, f32[16,4,32,256]{3,2,0,1:T(8,128)S(1)}, u32[]{:S(2)}) copy-start(f32[16,4,32,256]{3,2,0,1:T(8,128)S(1)} %copy.14) | copy-start | bytes 6291460
  75.7 7.8 %collective-permute-start = (f32[6,32,256]{2,1,0:T(8,128)S(1)}, f32[6,32,256]{2,1,0:T(8,128)S(1)}, u32[]{:S(2)}, u32[]{:S(2)}) collective-permute-start(f32[6,32,256]{2,1,0:T(8,128)S(1)} %get-tuple-element.10), channel_id=1, source_target_pairs={{0,8},{2,10},{4,12},{6,14},{8,16},{10,18},{12,20},{14,22},{16,24},... | collective-permute-start | bytes 589832 | tf_op jit(solution)/shard_map/ppermute | solution.py:207
  77.0 7.7 %collective-permute-start.1 = (f32[6,32,256]{2,1,0:T(8,128)S(1)}, f32[6,32,256]{2,1,0:T(8,128)S(1)}, u32[]{:S(2)}, u32[]{:S(2)}) collective-permute-start(f32[6,32,256]{2,1,0:T(8,128)S(1)} %get-tuple-element.9), channel_id=1, source_target_pairs={{8,0},{10,2},{12,4},{14,6},{16,8},{18,10},{20,12},{22,14},{24,16},... | collective-permute-start | bytes 589832 | tf_op jit(solution)/shard_map/ppermute | solution.py:207
  83.5 1.3 copy-start.16
  96.1 135.5 %collective-permute-start.3 = (f32[64,32,256]{2,1,0:T(8,128)}, f32[64,32,256]{2,1,0:T(8,128)}, u32[]{:S(2)}, u32[]{:S(2)}) collective-permute-start(f32[64,32,256]{2,1,0:T(8,128)} %shard_map.46.own), channel_id=1, source_target_pairs={{0,8},{2,10},{4,12},{6,14},{8,16},{10,18},{12,20},{14,22},{16,24},... | collective-permute-start | bytes 6291464 | tf_op jit(solution)/shard_map/ppermute | solution.py:207
  97.3 134.2 %collective-permute-start.4 = (f32[64,32,256]{2,1,0:T(8,128)}, f32[64,32,256]{2,1,0:T(8,128)}, u32[]{:S(2)}, u32[]{:S(2)}) collective-permute-start(f32[64,32,256]{2,1,0:T(8,128)} %shard_map.46.own), channel_id=1, source_target_pairs={{8,0},{10,2},{12,4},{14,6},{16,8},{18,10},{20,12},{22,14},{24,16},... | collective-permute-start | bytes 6291464 | tf_op jit(solution)/shard_map/ppermute | solution.py:207
  107.8 151.4 %all-to-all-start.6 = ((f32[16,128,256]{2,0,1:T(8,128)}), f32[16,128,256]{2,0,1:T(8,128)}, u32[]{:S(2)}, u32[]{:S(2)}) async-start(f32[16,128,256]{2,0,1:T(8,128)} %copy.28), calls=%async_computation.6 | async-start | bytes 4194304 | tf_op jit(solution)/shard_map/all_to_all | solution.py:212
  115.1 37.2 %copy-start.1 = (f32[16,4,32,256]{3,2,0,1:T(8,128)}, f32[16,4,32,256]{3,2,0,1:T(8,128)S(1)}, u32[]{:S(2)}) copy-start(f32[16,4,32,256]{3,2,0,1:T(8,128)S(1)} %copy.17) | copy-start | bytes 6291460
  115.2 33.5 %collective-permute-start.6 = (f32[6,32,256]{2,1,0:T(8,128)S(1)}, f32[6,32,256]{2,1,0:T(8,128)S(1)}, u32[]{:S(2)}, u32[]{:S(2)}) collective-permute-start(f32[6,32,256]{2,1,0:T(8,128)S(1)} %get-tuple-element.12), channel_id=1, source_target_pairs={{0,8},{2,10},{4,12},{6,14},{8,16},{10,18},{12,20},{14,22},{16,24},... | collective-permute-start | bytes 589832 | tf_op jit(solution)/shard_map/ppermute | solution.py:207
  116.5 35.9 %collective-permute-start.7 = (f32[6,32,256]{2,1,0:T(8,128)S(1)}, f32[6,32,256]{2,1,0:T(8,128)S(1)}, u32[]{:S(2)}, u32[]{:S(2)}) collective-permute-start(f32[6,32,256]{2,1,0:T(8,128)S(1)} %get-tuple-element.11), channel_id=1, source_target_pairs={{8,0},{10,2},{12,4},{14,6},{16,8},{18,10},{20,12},{22,14},{24,16},... | collective-permute-start | bytes 589832 | tf_op jit(solution)/shard_map/ppermute | solution.py:207
  122.0 53.9 %collective-permute-start.5 = (f32[7,32,256]{2,1,0:T(8,128)S(1)}, f32[7,32,256]{2,1,0:T(8,128)S(1)}, u32[]{:S(2)}, u32[]{:S(2)}) collective-permute-start(f32[7,32,256]{2,1,0:T(8,128)S(1)} %slice.83), channel_id=1, source_target_pairs={{16,0},{18,2},{20,4},{22,6},{24,8},{26,10},{28,12},{30,14},{17,1},... | collective-permute-start | bytes 688136 | tf_op jit(solution)/shard_map/ppermute | solution.py:207
  148.7 3.6 copy-start.18
  163.7 176.0 %collective-permute-start.10 = (f32[64,32,256]{2,1,0:T(8,128)}, f32[64,32,256]{2,1,0:T(8,128)}, u32[]{:S(2)}, u32[]{:S(2)}) collective-permute-start(f32[64,32,256]{2,1,0:T(8,128)} %shard_map.48.own), channel_id=1, source_target_pairs={{8,0},{10,2},{12,4},{14,6},{16,8},{18,10},{20,12},{22,14},{24,16},... | collective-permute-start | bytes 6291464 | tf_op jit(solution)/shard_map/ppermute | solution.py:207
  173.6 166.1 %collective-permute-start.9 = (f32[64,32,256]{2,1,0:T(8,128)}, f32[64,32,256]{2,1,0:T(8,128)}, u32[]{:S(2)}, u32[]{:S(2)}) collective-permute-start(f32[64,32,256]{2,1,0:T(8,128)} %shard_map.48.own), channel_id=1, source_target_pairs={{0,8},{2,10},{4,12},{6,14},{8,16},{10,18},{12,20},{14,22},{16,24},... | collective-permute-start | bytes 6291464 | tf_op jit(solution)/shard_map/ppermute | solution.py:207
  175.9 55.6 %copy-start.12 = (f32[7,32,256]{2,1,0:T(8,128)}, f32[7,32,256]{2,1,0:T(8,128)S(1)}, u32[]{:S(2)}) copy-start(f32[7,32,256]{2,1,0:T(8,128)S(1)} %collective-permute-done.5.far_hi) | copy-start | bytes 688132
  175.9 55.6 %collective-permute-start.2 = (f32[13,32,256]{2,1,0:T(8,128)S(1)}, f32[13,32,256]{2,1,0:T(8,128)S(1)}, u32[]{:S(2)}, u32[]{:S(2)}) collective-permute-start(f32[13,32,256]{2,1,0:T(8,128)S(1)} %slice.82), channel_id=1, source_target_pairs={{0,16},{2,18},{4,20},{6,22},{8,24},{10,26},{12,28},{14,30},{1,17},... | collective-permute-start | bytes 1277960 | tf_op jit(solution)/shard_map/ppermute | solution.py:207
  231.5 0.8 copy-start.9
  259.3 108.1 %all-to-all-start.1 = ((f32[64,32,256]{2,1,0:T(8,128)}), f32[64,32,256]{2,1,0:T(8,128)}, u32[]{:S(2)}, u32[]{:S(2)}) async-start(f32[64,32,256]{2,1,0:T(8,128)} %shard_map.47), calls=%async_computation.1 | async-start | bytes 4194304 | tf_op jit(solution)/shard_map/all_to_all | solution.py:225
  266.7 9.1 %copy-start.2 = (f32[16,4,32,256]{3,2,0,1:T(8,128)}, f32[16,4,32,256]{3,2,0,1:T(8,128)S(1)}, u32[]{:S(2)}) copy-start(f32[16,4,32,256]{3,2,0,1:T(8,128)S(1)} %copy.20) | copy-start | bytes 6291460
  266.8 8.3 %collective-permute-start.12 = (f32[6,32,256]{2,1,0:T(8,128)S(1)}, f32[6,32,256]{2,1,0:T(8,128)S(1)}, u32[]{:S(2)}, u32[]{:S(2)}) collective-permute-start(f32[6,32,256]{2,1,0:T(8,128)S(1)} %get-tuple-element.14), channel_id=1, source_target_pairs={{0,8},{2,10},{4,12},{6,14},{8,16},{10,18},{12,20},{14,22},{16,24},... | collective-permute-start | bytes 589832 | tf_op jit(solution)/shard_map/ppermute | solution.py:207
  268.1 7.7 %collective-permute-start.13 = (f32[6,32,256]{2,1,0:T(8,128)S(1)}, f32[6,32,256]{2,1,0:T(8,128)S(1)}, u32[]{:S(2)}, u32[]{:S(2)}) collective-permute-start(f32[6,32,256]{2,1,0:T(8,128)S(1)} %get-tuple-element.13), channel_id=1, source_target_pairs={{8,0},{10,2},{12,4},{14,6},{16,8},{18,10},{20,12},{22,14},{24,16},... | collective-permute-start | bytes 589832 | tf_op jit(solution)/shard_map/ppermute | solution.py:207
  273.6 22.2 %collective-permute-start.11 = (f32[7,32,256]{2,1,0:T(8,128)S(1)}, f32[7,32,256]{2,1,0:T(8,128)S(1)}, u32[]{:S(2)}, u32[]{:S(2)}) collective-permute-start(f32[7,32,256]{2,1,0:T(8,128)S(1)} %slice.87), channel_id=1, source_target_pairs={{16,0},{18,2},{20,4},{22,6},{24,8},{26,10},{28,12},{30,14},{17,1},... | collective-permute-start | bytes 688136 | tf_op jit(solution)/shard_map/ppermute | solution.py:207
  287.2 155.3 %collective-permute-start.15 = (f32[64,32,256]{2,1,0:T(8,128)}, f32[64,32,256]{2,1,0:T(8,128)}, u32[]{:S(2)}, u32[]{:S(2)}) collective-permute-start(f32[64,32,256]{2,1,0:T(8,128)} %shard_map.50.own), channel_id=1, source_target_pairs={{0,8},{2,10},{4,12},{6,14},{8,16},{10,18},{12,20},{14,22},{16,24},... | collective-permute-start | bytes 6291464 | tf_op jit(solution)/shard_map/ppermute | solution.py:207
  288.5 154.0 %collective-permute-start.16 = (f32[64,32,256]{2,1,0:T(8,128)}, f32[64,32,256]{2,1,0:T(8,128)}, u32[]{:S(2)}, u32[]{:S(2)}) collective-permute-start(f32[64,32,256]{2,1,0:T(8,128)} %shard_map.50.own), channel_id=1, source_target_pairs={{8,0},{10,2},{12,4},{14,6},{16,8},{18,10},{20,12},{22,14},{24,16},... | collective-permute-start | bytes 6291464 | tf_op jit(solution)/shard_map/ppermute | solution.py:207
  295.9 43.8 %copy-start.13 = (f32[7,32,256]{2,1,0:T(8,128)}, f32[7,32,256]{2,1,0:T(8,128)S(1)}, u32[]{:S(2)}) copy-start(f32[7,32,256]{2,1,0:T(8,128)S(1)} %collective-permute-done.11.far_hi) | copy-start | bytes 688132
  295.9 43.8 %collective-permute-start.8 = (f32[13,32,256]{2,1,0:T(8,128)S(1)}, f32[13,32,256]{2,1,0:T(8,128)S(1)}, u32[]{:S(2)}, u32[]{:S(2)}) collective-permute-start(f32[13,32,256]{2,1,0:T(8,128)S(1)} %slice.86), channel_id=1, source_target_pairs={{0,16},{2,18},{4,20},{6,22},{8,24},{10,26},{12,28},{14,30},{1,17},... | collective-permute-start | bytes 1277960 | tf_op jit(solution)/shard_map/ppermute | solution.py:207
  367.4 102.9 %all-to-all-start.3 = ((f32[64,32,256]{2,1,0:T(8,128)}), f32[64,32,256]{2,1,0:T(8,128)}, u32[]{:S(2)}, u32[]{:S(2)}) async-start(f32[64,32,256]{2,1,0:T(8,128)} %shard_map.49), calls=%async_computation.3 | async-start | bytes 4194304 | tf_op jit(solution)/shard_map/all_to_all | solution.py:225
  374.7 11.2 %copy-start.3 = (f32[16,4,32,256]{3,2,0,1:T(8,128)}, f32[16,4,32,256]{3,2,0,1:T(8,128)S(1)}, u32[]{:S(2)}) copy-start(f32[16,4,32,256]{3,2,0,1:T(8,128)S(1)} %copy.23) | copy-start | bytes 6291460
  374.7 9.7 %collective-permute-start.18 = (f32[6,32,256]{2,1,0:T(8,128)S(1)}, f32[6,32,256]{2,1,0:T(8,128)S(1)}, u32[]{:S(2)}, u32[]{:S(2)}) collective-permute-start(f32[6,32,256]{2,1,0:T(8,128)S(1)} %get-tuple-element.16), channel_id=1, source_target_pairs={{0,8},{2,10},{4,12},{6,14},{8,16},{10,18},{12,20},{14,22},{16,24},... | collective-permute-start | bytes 589832 | tf_op jit(solution)/shard_map/ppermute | solution.py:207
  376.0 9.8 %collective-permute-start.19 = (f32[6,32,256]{2,1,0:T(8,128)S(1)}, f32[6,32,256]{2,1,0:T(8,128)S(1)}, u32[]{:S(2)}, u32[]{:S(2)}) collective-permute-start(f32[6,32,256]{2,1,0:T(8,128)S(1)} %get-tuple-element.15), channel_id=1, source_target_pairs={{8,0},{10,2},{12,4},{14,6},{16,8},{18,10},{20,12},{22,14},{24,16},... | collective-permute-start | bytes 589832 | tf_op jit(solution)/shard_map/ppermute | solution.py:207
  381.5 24.3 %collective-permute-start.17 = (f32[7,32,256]{2,1,0:T(8,128)S(1)}, f32[7,32,256]{2,1,0:T(8,128)S(1)}, u32[]{:S(2)}, u32[]{:S(2)}) collective-permute-start(f32[7,32,256]{2,1,0:T(8,128)S(1)} %slice.91), channel_id=1, source_target_pairs={{16,0},{18,2},{20,4},{22,6},{24,8},{26,10},{28,12},{30,14},{17,1},... | collective-permute-start | bytes 688136 | tf_op jit(solution)/shard_map/ppermute | solution.py:207
  384.4 1.5 copy-start.20
  397.2 89.3 %collective-permute-start.21 = (f32[64,32,256]{2,1,0:T(8,128)}, f32[64,32,256]{2,1,0:T(8,128)}, u32[]{:S(2)}, u32[]{:S(2)}) collective-permute-start(f32[64,32,256]{2,1,0:T(8,128)} %shard_map.52.own), channel_id=1, source_target_pairs={{0,8},{2,10},{4,12},{6,14},{8,16},{10,18},{12,20},{14,22},{16,24},... | collective-permute-start | bytes 6291464 | tf_op jit(solution)/shard_map/ppermute | solution.py:207
  398.4 88.0 %collective-permute-start.22 = (f32[64,32,256]{2,1,0:T(8,128)}, f32[64,32,256]{2,1,0:T(8,128)}, u32[]{:S(2)}, u32[]{:S(2)}) collective-permute-start(f32[64,32,256]{2,1,0:T(8,128)} %shard_map.52.own), channel_id=1, source_target_pairs={{8,0},{10,2},{12,4},{14,6},{16,8},{18,10},{20,12},{22,14},{24,16},... | collective-permute-start | bytes 6291464 | tf_op jit(solution)/shard_map/ppermute | solution.py:207
  405.8 36.7 %copy-start.14 = (f32[7,32,256]{2,1,0:T(8,128)}, f32[7,32,256]{2,1,0:T(8,128)S(1)}, u32[]{:S(2)}) copy-start(f32[7,32,256]{2,1,0:T(8,128)S(1)} %collective-permute-done.17.far_hi) | copy-start | bytes 688132
  405.8 36.7 %collective-permute-start.14 = (f32[13,32,256]{2,1,0:T(8,128)S(1)}, f32[13,32,256]{2,1,0:T(8,128)S(1)}, u32[]{:S(2)}, u32[]{:S(2)}) collective-permute-start(f32[13,32,256]{2,1,0:T(8,128)S(1)} %slice.90), channel_id=1, source_target_pairs={{0,16},{2,18},{4,20},{6,22},{8,24},{10,26},{12,28},{14,30},{1,17},... | collective-permute-start | bytes 1277960 | tf_op jit(solution)/shard_map/ppermute | solution.py:207
  470.3 44.0 %all-to-all-start.5 = ((f32[64,32,256]{2,1,0:T(8,128)}), f32[64,32,256]{2,1,0:T(8,128)S(1)}, u32[]{:S(2)}, u32[]{:S(2)}) async-start(f32[64,32,256]{2,1,0:T(8,128)} %shard_map.51), calls=%async_computation.5 | async-start | bytes 4194304 | tf_op jit(solution)/shard_map/all_to_all | solution.py:225
  475.2 11.3 %collective-permute-start.20 = (f32[13,32,256]{2,1,0:T(8,128)S(1)}, f32[13,32,256]{2,1,0:T(8,128)S(1)}, u32[]{:S(2)}, u32[]{:S(2)}) collective-permute-start(f32[13,32,256]{2,1,0:T(8,128)S(1)} %slice.94), channel_id=1, source_target_pairs={{0,16},{2,18},{4,20},{6,22},{8,24},{10,26},{12,28},{14,30},{1,17},... | collective-permute-start | bytes 1277960 | tf_op jit(solution)/shard_map/ppermute | solution.py:207
  477.5 9.0 %collective-permute-start.23 = (f32[7,32,256]{2,1,0:T(8,128)S(1)}, f32[7,32,256]{2,1,0:T(8,128)S(1)}, u32[]{:S(2)}, u32[]{:S(2)}) collective-permute-start(f32[7,32,256]{2,1,0:T(8,128)S(1)} %slice.95), channel_id=1, source_target_pairs={{16,0},{18,2},{20,4},{22,6},{24,8},{26,10},{28,12},{30,14},{17,1},... | collective-permute-start | bytes 688136 | tf_op jit(solution)/shard_map/ppermute | solution.py:207
  486.5 0.8 copy-start.8
  514.2 19.6 %all-to-all-start.7 = ((f32[64,32,256]{2,1,0:T(8,128)}), f32[64,32,256]{2,1,0:T(8,128)}, u32[]{:S(2)}, u32[]{:S(2)}) async-start(f32[64,32,256]{2,1,0:T(8,128)} %shard_map.53), calls=%async_computation.7 | async-start | bytes 4194304 | tf_op jit(solution)/shard_map/all_to_all | solution.py:225
  533.8 2.2 copy-start.6
  533.8 2.9 copy-start.7
  (8 other events, 5.6 us)

commit v2 on v0

v2 whole, which is shorter than its diff:
```python
import functools

import jax
import jax.numpy as jnp
from jax import lax
from jax.experimental import pallas as pl
from jax.experimental.pallas import tpu as pltpu
from jax.sharding import PartitionSpec as P

SWEEPS = 6
DIFFUSE = 6
BAND = 8
STEP_SIZE = 0.24
LEVEL_SCALE = 16.0
LANES = 128
ROWS = 8
LEAD = 4
FAR_LO = DIFFUSE + BAND - 1
FAR_HI = DIFFUSE + 1
MESH = pl.DeviceIdType.MESH


def sweep_pass(src, dst, dst_from, n_in, n_out, sweeps, inverse, tiles):
    lead = (n_in - n_out) // 2 + 2 * sweeps - 1

    def advance(t, carry):
        held, flux, made = carry
        at = jnp.minimum(t, n_in - 1)
        new_held, new_flux, new_made = [], [], []
        for s, tile in enumerate(tiles):
            fresh = src[at, tile, :]
            for level in range(sweeps):
                k = s * sweeps + level
                b = fresh if level == 0 else made[k - 1]
                a = held[k]
                c = b - a
                cc = c * c if inverse is None else c * c * inverse[s]
                f = c / (1.0 + cc)
                new_made.append(a + STEP_SIZE * (f - flux[k]))
                new_held.append(b)
                new_flux.append(f)
        return tuple(new_held), tuple(new_flux), tuple(new_made)

    def work(t, carry):
        carry = advance(t + lead, carry)
        for s, tile in enumerate(tiles):
            dst[dst_from + t, tile, :] = carry[2][s * sweeps + sweeps - 1]
        return carry

    start = tuple(src[0, tile, :] for tile in tiles for _ in range(sweeps))
    carry = lax.fori_loop(0, lead, advance, (start, start, start))
    lax.fori_loop(0, n_out, work, carry)


def kernel(group, chunks, off_ref, bw_ref, x, edge, out, *scratch):
    wins = scratch[:chunks]
    (raw, made, prof, edge_v, in_send, in_recv, in_own, halo_send, halo_recv,
     far_send, far_recv, out_send, out_recv, out_own, edge_sem) = scratch[chunks:]
    local = x.shape[0]
    rows = x.shape[1] // group
    frames = local * group
    all_frames = frames * LEAD
    own_at = FAR_LO + frames
    me = lax.axis_index("scan")
    k = lax.rem(me, group)
    z = lax.div(me, group)
    tile_count = rows // ROWS
    pair = 2 if tile_count % 2 == 0 else 1

    def rows_of(j):
        return pl.ds(pl.multiple_of(j * rows, ROWS), rows)

    def cols_of(c):
        return pl.ds(c * LANES, LANES)

    def mate(m):
        return z * group + lax.rem(k + m, group)

    has = {1: z < LEAD - 1, -1: z > 0, 2: z < LEAD - 2, -2: z > 1}

    barrier = pltpu.get_barrier_semaphore()
    for m in range(1, group):
        pl.semaphore_signal(barrier, inc=1, device_id={"scan": mate(m)}, device_id_type=MESH)
    for step, there in has.items():

        @pl.when(there)
        def _(step=step):
            pl.semaphore_signal(
                barrier, inc=1, device_id={"scan": me + step * group}, device_id_type=MESH
            )

    count = group - 1
    for there in has.values():
        count = count + there.astype(jnp.int32)
    pl.semaphore_wait(barrier, count)

    def in_copy(c, m):
        return pltpu.make_async_remote_copy(
            src_ref=x.at[:, rows_of(lax.rem(k + m, group)), cols_of(c)],
            dst_ref=raw.at[c, pl.ds(SWEEPS + k * local, local)],
            send_sem=in_send.at[c, m - 1],
            recv_sem=in_recv.at[c, m - 1],
            device_id={"scan": mate(m)},
            device_id_type=MESH,
        )

    def in_local(c):
        return pltpu.make_async_copy(
            x.at[:, rows_of(k), cols_of(c)],
            raw.at[c, pl.ds(SWEEPS + k * local, local)],
            in_own.at[c],
        )

    def out_copy(c, m):
        return pltpu.make_async_remote_copy(
            src_ref=made.at[c, pl.ds(lax.rem(k + m, group) * local, local)],
            dst_ref=out.at[:, rows_of(k), cols_of(c)],
            send_sem=out_send.at[c, m - 1],
            recv_sem=out_recv.at[c, m - 1],
            device_id={"scan": mate(m)},
            device_id_type=MESH,
        )

    def out_local(c):
        return pltpu.make_async_copy(
            made.at[c, pl.ds(k * local, local)],
            out.at[:, rows_of(k), cols_of(c)],
            out_own.at[c],
        )

    def z_copy(src, dst, sems, c, i, step):
        send, recv = sems
        return pltpu.make_async_remote_copy(
            src_ref=src,
            dst_ref=dst,
            send_sem=send.at[c, i],
            recv_sem=recv.at[c, i],
            device_id={"scan": me + step * group},
            device_id_type=MESH,
        )

    def halo_copies(c):
        sems = (halo_send, halo_recv)
        up = z_copy(raw.at[c, pl.ds(frames, SWEEPS)], raw.at[c, pl.ds(0, SWEEPS)], sems, c, 0, 1)
        down = z_copy(
            raw.at[c, pl.ds(SWEEPS, SWEEPS)],
            raw.at[c, pl.ds(SWEEPS + frames, SWEEPS)], sems, c, 1, -1,
        )
        return ((1, up), (-1, down))

    def far_copies(c):
        win, sems = wins[c], (far_send, far_recv)
        own = win.at[pl.ds(own_at, frames)]
        return (
            (1, z_copy(own, win.at[pl.ds(FAR_LO, frames)], sems, c, 0, 1)),
            (-1, z_copy(own, win.at[pl.ds(own_at + frames, frames)], sems, c, 1, -1)),
            (2, z_copy(win.at[pl.ds(own_at + frames - FAR_LO, FAR_LO)],
                       win.at[pl.ds(0, FAR_LO)], sems, c, 2, 2)),
            (-2, z_copy(win.at[pl.ds(own_at, FAR_HI)],
                        win.at[pl.ds(own_at + 2 * frames, FAR_HI)], sems, c, 3, -2)),
        )

    def start(copies):
        for step, copy in copies:
            pl.when(has[step])(copy.start)

    def wait_recv(copies):
        for step, copy in copies:
            pl.when(has[-step])(copy.wait_recv)

    def wait_send(copies):
        for step, copy in copies:
            pl.when(has[step])(copy.wait_send)

    edge_copy = pltpu.make_async_copy(edge.at[rows_of(k)], edge_v, edge_sem)
    for c in range(chunks):
        in_local(c).start()
        for m in range(1, group):
            in_copy(c, m).start()
    edge_copy.start()

    def arrive(c):
        in_local(c).wait()
        for m in range(1, group):
            in_copy(c, m).wait_recv()
        start(halo_copies(c))

    def smooth(c):
        wait_recv(halo_copies(c))

        @pl.when(z == 0)
        def _():
            for i in range(SWEEPS):
                raw[c, i] = raw[c, 2 * SWEEPS - 1 - i]

        @pl.when(z == LEAD - 1)
        def _():
            for i in range(SWEEPS):
                raw[c, SWEEPS + frames + i] = raw[c, SWEEPS + frames - 1 - i]

        def one(p, _):
            tiles = [pl.ds(pl.multiple_of((p * pair + s) * ROWS, ROWS), ROWS) for s in range(pair)]
            sweep_pass(
                raw.at[c], wins[c], own_at, frames + 2 * SWEEPS, frames, SWEEPS, None, tiles
            )
            return 0

        lax.fori_loop(0, tile_count // pair, one, 0)
        start(far_copies(c))

    def repeat(win, first, count, source):
        def one(i, _):
            win[first + i] = win[source]
            return 0

        lax.fori_loop(0, count, one, 0)

    def depth(c):
        win = wins[c]
        wait_recv(far_copies(c))
        pl.when(z == 0)(lambda: repeat(win, 0, own_at, own_at))
        pl.when(z == 1)(lambda: repeat(win, 0, FAR_LO, FAR_LO))
        end = own_at + frames
        pl.when(z == LEAD - 1)(lambda: repeat(win, end, frames + FAR_HI, end - 1))
        pl.when(z == LEAD - 2)(lambda: repeat(win, end + frames, FAR_HI, end + frames - 1))
        sub = lax.broadcasted_iota(jnp.int32, (ROWS, LANES), 0)

        def one_tile(p, _):
            tile = pl.ds(pl.multiple_of(p * ROWS, ROWS), ROWS)
            row0 = k * rows + p * ROWS
            at_b = [own_at - z * frames + 1 - off_ref[row0 + r] for r in range(ROWS)]
            bws = [bw_ref[row0 + r] for r in range(ROWS)]
            at_a = [at_b[r] - bws[r] for r in range(ROWS)]
            widths = jnp.where(sub == 0, bws[0].astype(jnp.float32), 1.0)
            for r in range(1, ROWS):
                widths = jnp.where(sub == r, bws[r].astype(jnp.float32), widths)

            def fill(d, _):
                at = z * frames + d - DIFFUSE
                at = jnp.where(at < 0, -1 - at, at)
                at = jnp.where(at >= all_frames, 2 * all_frames - 1 - at, at)
                a = win[at + at_a[0], tile, :]
                b = win[at + at_b[0], tile, :]
                for r in range(1, ROWS):
                    a = jnp.where(sub == r, win[at + at_a[r], tile, :], a)
                    b = jnp.where(sub == r, win[at + at_b[r], tile, :], b)
                prof[d, tile, :] = (a - b) / widths
                return 0

            lax.fori_loop(0, frames + 2 * DIFFUSE, fill, 0)
            return 0

        lax.fori_loop(0, tile_count, one_tile, 0)

        def one(p, _):
            tiles = [pl.ds(pl.multiple_of((p * pair + s) * ROWS, ROWS), ROWS) for s in range(pair)]
            inverse = []
            for tile in tiles:
                level = edge_v[tile, pl.ds(c * LANES, LANES)].astype(jnp.float32) / LEVEL_SCALE
                inverse.append(1.0 / (level * level))
            sweep_pass(
                prof, made.at[c], 0, frames + 2 * DIFFUSE, frames, DIFFUSE, inverse, tiles
            )
            return 0

        lax.fori_loop(0, tile_count // pair, one, 0)
        out_local(c).start()
        for m in range(1, group):
            out_copy(c, m).start()

    arrive(0)
    for c in range(chunks):
        if c + 1 < chunks:
            arrive(c + 1)
        smooth(c)
        if c == 0:
            edge_copy.wait()
        else:
            depth(c - 1)
    depth(chunks - 1)
    for c in range(chunks):
        for m in range(1, group):
            in_copy(c, m).wait_send()
        wait_send(halo_copies(c))
        wait_send(far_copies(c))
        out_local(c).wait()
        for m in range(1, group):
            out_copy(c, m).wait()


def body(frames, depth_offset, band_width, edge_level):
    group = lax.axis_size("scan") // LEAD
    local, all_rows, cols = frames.shape
    chunks, rows, block = cols // LANES, all_rows // group, local * group
    dma = pltpu.SemaphoreType.DMA
    smem = pl.BlockSpec(memory_space=pltpu.SMEM)
    anywhere = pl.BlockSpec(memory_space=pl.ANY)
    win = pltpu.VMEM((3 * block + FAR_LO + FAR_HI, rows, LANES), jnp.float32)
    return pl.pallas_call(
        functools.partial(kernel, group, chunks),
        out_shape=jax.ShapeDtypeStruct(frames.shape, frames.dtype),
        in_specs=[smem, smem, anywhere, anywhere],
        out_specs=anywhere,
        scratch_shapes=[win] * chunks
        + [
            pltpu.VMEM((chunks, block + 2 * SWEEPS, rows, LANES), jnp.float32),
            pltpu.VMEM((chunks, block, rows, LANES), jnp.float32),
            pltpu.VMEM((block + 2 * DIFFUSE, rows, LANES), jnp.float32),
            pltpu.VMEM((rows, cols), jnp.int32),
            dma((chunks, group - 1)),
            dma((chunks, group - 1)),
            dma((chunks,)),
            dma((chunks, 2)),
            dma((chunks, 2)),
            dma((chunks, 4)),
            dma((chunks, 4)),
            dma((chunks, group - 1)),
            dma((chunks, group - 1)),
            dma((chunks,)),
            dma,
        ],
        compiler_params=pltpu.CompilerParams(
            collective_id=0, has_side_effects=True, vmem_limit_bytes=60 * 1024 * 1024
        ),
    )(depth_offset, band_width, frames, edge_level)


def solution(mesh):
    placed = (P("scan", None, "col"), P(), P(), P(None, "col"))
    return jax.shard_map(
        body, mesh=mesh, in_specs=placed, out_specs=P("scan", None, "col"), check_vma=False
    )
```

time: 776 us -> 334 us (0.43); the launches traced: 767 us -> 334 us
  waiting for transfers between devices: 464 us -> 0 us
  Pallas kernels: 0 us -> 325 us
  other arithmetic: 161 us -> 0 us
  starting transfers between devices: 70.1 us -> 0 us
  local copies, waits for them, and re-layouts: 58.1 us -> 8.44 us
  matrix products: 12.3 us -> 0 us
    all_to_all x2 -> x0, waiting for transfers between devices: 359 us -> none  [the longest x1 180 us: body(): lax.all_to_all(frames, 'scan', split_axis=1, concat_axis=0, tiled=True)]
    pallas_call x0 -> x1, Pallas kernels: none -> 325 us  [body(): pl.pallas_call(functools.partial(kernel, group, chunks), out_shape=jax.Sh...]
    ppermute x12 -> x0, waiting for transfers between devices: 106 us -> none  [the longest x6 67.3 us: with_halo(): after = lax.ppermute(initial, axis, down)]
    add x12 -> x0, other arithmetic: 92.4 us -> none  [diffuse_once(): field + STEP_SIZE * (jnp.concatenate([flux_out, zero_row], 0) - jnp.conca...]
    div x13 -> x0, other arithmetic: 57.3 us -> none  [the longest x12 57.2 us: diffuse_once(): flux_out = change / (1.0 + change * change / (kappa * kappa))]
    ppermute x12 -> x0, starting transfers between devices: 46.7 us -> none  [the longest x6 34 us: with_halo(): after = lax.ppermute(initial, axis, down)]
    all_to_all x3 -> x0, local copies, waits for them, and re-layouts: 27.4 us -> none  [the longest x2 23.1 us: body(): lax.all_to_all(frames, 'scan', split_axis=1, concat_axis=0, tiled=True)]
    all_to_all x2 -> x0, starting transfers between devices: 23.5 us -> none  [the longest x1 16 us: body(): lax.all_to_all(profile, 'scan', split_axis=0, concat_axis=1, tiled=True)]
  transfers between devices with their start and end apart: 14 -> 0, of which waited for: 14 -> 0; matrix products, arithmetic and copies ran while one was open for 2% -> 0% of each run, Pallas kernels for 0% -> 0%
where the time goes in v2:
time: 334 us
  Pallas kernels  325 us (97%)
  local copies, waits for them, and re-layouts  8.44 us (3%)
    pallas_call x1, Pallas kernels, body(): pl.pallas_call(functools.partial(kernel, group, chunks), out_shape=jax.Sh...  325 us
    unnamed x1, local copies, waits for them, and re-layouts  8.44 us

profile of v2, /device:TPU:24, one launch (start us, length us, event | category | flops | bytes accessed | tf_op | source)
XLA Modules:
  0.0 333.8 jit_solution(5685726049255562914)
XLA Ops:
  0.0 325.3 %shard_map.46 = f32[16,128,1024]{2,1,0:T(8,128)} custom-call(s32[128]{0:T(128)} %off_ref.1, s32[128]{0:T(128)} %bw_ref.1, f32[16,128,1024]{2,1,0:T(8,128)} %x.1, s32[128,1024]{1,0:T(8,128)} %edge.1), custom_call_target="tpu_custom_call" | custom-call | tf_op jit(solution)/shard_map/pallas_call | solution.py:299
  325.3 8.4 %copy.6 = f32[16,128,1024]{2,1,0:T(8,128)} copy(f32[16,128,1024]{2,1,0:T(8,128)} %shard_map.46) | data formatting | bytes 16777216

commit v3 on v2

--- a/solution.py
+++ b/solution.py
@@ -17,6 +17,7 @@
 LEAD = 4
 FAR_LO = DIFFUSE + BAND - 1
 FAR_HI = DIFFUSE + 1
+LAG = 2
 MESH = pl.DeviceIdType.MESH
 
 
@@ -35,7 +36,9 @@
                 a = held[k]
                 c = b - a
                 cc = c * c if inverse is None else c * c * inverse[s]
-                f = c / (1.0 + cc)
+                d = 1.0 + cc
+                q = pl.reciprocal(d, approx=True)
+                f = c * (q * (2.0 - d * q))
                 new_made.append(a + STEP_SIZE * (f - flux[k]))
                 new_held.append(b)
                 new_flux.append(f)
@@ -49,7 +52,7 @@
 
     start = tuple(src[0, tile, :] for tile in tiles for _ in range(sweeps))
     carry = lax.fori_loop(0, lead, advance, (start, start, start))
-    lax.fori_loop(0, n_out, work, carry)
+    lax.fori_loop(0, n_out, work, carry, unroll=2)
 
 
 def kernel(group, chunks, off_ref, bw_ref, x, edge, out, *scratch):
@@ -76,22 +79,24 @@
     def mate(m):
         return z * group + lax.rem(k + m, group)
 
-    has = {1: z < LEAD - 1, -1: z > 0, 2: z < LEAD - 2, -2: z > 1}
+    inner = jnp.logical_and(z > 0, z < LEAD - 1)
+    has = {1: z < LEAD - 1, -1: z > 0, 2: inner, -2: inner}
+    gets = {1: z > 0, -1: z < LEAD - 1, 2: z > 1, -2: z < LEAD - 2}
 
     barrier = pltpu.get_barrier_semaphore()
     for m in range(1, group):
         pl.semaphore_signal(barrier, inc=1, device_id={"scan": mate(m)}, device_id_type=MESH)
-    for step, there in has.items():
-
-        @pl.when(there)
+    for step in (1, -1):
+
+        @pl.when(has[step])
         def _(step=step):
             pl.semaphore_signal(
                 barrier, inc=1, device_id={"scan": me + step * group}, device_id_type=MESH
             )
 
     count = group - 1
-    for there in has.values():
-        count = count + there.astype(jnp.int32)
+    for step in (1, -1):
+        count = count + has[step].astype(jnp.int32)
     pl.semaphore_wait(barrier, count)
 
     def in_copy(c, m):
@@ -148,17 +153,32 @@
         )
         return ((1, up), (-1, down))
 
+    def near_copies(c, first):
+        win, end = wins[c], own_at + frames
+
+        def one(src, dst, count, i, step):
+            return z_copy(
+                win.at[pl.ds(src, count)], win.at[pl.ds(dst, count)], (far_send, far_recv), c, i, step
+            )
+
+        if first:
+            return (
+                (1, one(end - FAR_LO, own_at - FAR_LO, FAR_LO, 0, 1)),
+                (-1, one(own_at, end, FAR_HI, 1, -1)),
+            )
+        return (
+            (1, one(own_at, FAR_LO, frames - FAR_LO, 2, 1)),
+            (-1, one(own_at + FAR_HI, end + FAR_HI, frames - FAR_HI, 3, -1)),
+        )
+
     def far_copies(c):
-        win, sems = wins[c], (far_send, far_recv)
-        own = win.at[pl.ds(own_at, frames)]
-        return (
-            (1, z_copy(own, win.at[pl.ds(FAR_LO, frames)], sems, c, 0, 1)),
-            (-1, z_copy(own, win.at[pl.ds(own_at + frames, frames)], sems, c, 1, -1)),
-            (2, z_copy(win.at[pl.ds(own_at + frames - FAR_LO, FAR_LO)],
-                       win.at[pl.ds(0, FAR_LO)], sems, c, 2, 2)),
-            (-2, z_copy(win.at[pl.ds(own_at, FAR_HI)],
-                        win.at[pl.ds(own_at + 2 * frames, FAR_HI)], sems, c, 3, -2)),
-        )
+        win, end = wins[c], own_at + frames
+        sems = (far_send, far_recv)
+        up = z_copy(win.at[pl.ds(own_at - FAR_LO, FAR_LO)], win.at[pl.ds(0, FAR_LO)], sems, c, 4, 1)
+        down = z_copy(
+            win.at[pl.ds(end, FAR_HI)], win.at[pl.ds(end + frames, FAR_HI)], sems, c, 5, -1
+        )
+        return ((2, up), (-2, down))
 
     def start(copies):
         for step, copy in copies:
@@ -166,7 +186,7 @@
 
     def wait_recv(copies):
         for step, copy in copies:
-            pl.when(has[-step])(copy.wait_recv)
+            pl.when(gets[step])(copy.wait_recv)
 
     def wait_send(copies):
         for step, copy in copies:
@@ -206,6 +226,11 @@
             return 0
 
         lax.fori_loop(0, tile_count // pair, one, 0)
+        start(near_copies(c, True))
+        start(near_copies(c, False))
+
+    def forward(c):
+        wait_recv(near_copies(c, True))
         start(far_copies(c))
 
     def repeat(win, first, count, source):
@@ -217,6 +242,7 @@
 
     def depth(c):
         win = wins[c]
+        wait_recv(near_copies(c, False))
         wait_recv(far_copies(c))
         pl.when(z == 0)(lambda: repeat(win, 0, own_at, own_at))
         pl.when(z == 1)(lambda: repeat(win, 0, FAR_LO, FAR_LO))
@@ -247,7 +273,7 @@
                 prof[d, tile, :] = (a - b) / widths
                 return 0
 
-            lax.fori_loop(0, frames + 2 * DIFFUSE, fill, 0)
+            lax.fori_loop(0, frames + 2 * DIFFUSE, fill, 0, unroll=4)
             return 0
 
         lax.fori_loop(0, tile_count, one_tile, 0)
@@ -272,16 +298,23 @@
     for c in range(chunks):
         if c + 1 < chunks:
             arrive(c + 1)
+        if c >= 1:
+            forward(c - 1)
         smooth(c)
         if c == 0:
             edge_copy.wait()
-        else:
-            depth(c - 1)
-    depth(chunks - 1)
+        if c >= LAG:
+            depth(c - LAG)
+    for c in range(max(chunks - LAG, 0), chunks):
+        if c == chunks - 1:
+            forward(c)
+        depth(c)
     for c in range(chunks):
         for m in range(1, group):
             in_copy(c, m).wait_send()
         wait_send(halo_copies(c))
+        wait_send(near_copies(c, True))
+        wait_send(near_copies(c, False))
         wait_send(far_copies(c))
         out_local(c).wait()
         for m in range(1, group):
@@ -312,8 +345,8 @@
             dma((chunks,)),
             dma((chunks, 2)),
             dma((chunks, 2)),
-            dma((chunks, 4)),
-            dma((chunks, 4)),
+            dma((chunks, 6)),
+            dma((chunks, 6)),
             dma((chunks, group - 1)),
             dma((chunks, group - 1)),
             dma((chunks,)),

time: 334 us -> 298 us (0.89)
  Pallas kernels: 325 us -> 288 us
    pallas_call x1, Pallas kernels: 325 us -> 288 us  [body(): pl.pallas_call(functools.partial(kernel, group, chunks), out_shape=jax.Sh...]
where the time goes in v3:
time: 298 us; the launch traced here: 296 us
  Pallas kernels  288 us (97%)
  local copies, waits for them, and re-layouts  8.44 us (3%)
    pallas_call x1, Pallas kernels, body(): pl.pallas_call(functools.partial(kernel, group, chunks), out_shape=jax.Sh...  288 us
    unnamed x1, local copies, waits for them, and re-layouts  8.44 us

profile of v3, /device:TPU:24, one launch (start us, length us, event | category | flops | bytes accessed | tf_op | source)
XLA Modules:
  0.0 296.3 jit_solution(5200620589258197792)
XLA Ops:
  0.0 287.8 %shard_map.46 = f32[16,128,1024]{2,1,0:T(8,128)} custom-call(s32[128]{0:T(128)} %off_ref.1, s32[128]{0:T(128)} %bw_ref.1, f32[16,128,1024]{2,1,0:T(8,128)} %x.1, s32[128,1024]{1,0:T(8,128)} %edge.1), custom_call_target="tpu_custom_call" | custom-call | tf_op jit(solution)/shard_map/pallas_call | solution.py:332
  287.8 8.4 %copy.6 = f32[16,128,1024]{2,1,0:T(8,128)} copy(f32[16,128,1024]{2,1,0:T(8,128)} %shard_map.46) | data formatting | bytes 16777216
